TPU v7x, 32 devices: a whole 2x2x4 slice. The times are simulated.
32 devices in a mesh: frame: 2 (over x), depth: 4 (over z), row: 4 (over y, core).
Axes of the slice: x: 2, y: 2, z: 4, core: 2. Of those that a mesh axis runs over, the one named last changes fastest.
Arguments:
- volume: bfloat16 [4, 2, 8, 18432], P('depth', 'frame', 'row'), may hold values from -6 to 6
- point_spread: bfloat16 [4, 576, 25, 144], P('depth', 'frame', None, 'row'), may hold values from -0.046875 to 0.046875
- region_map: int32 [8, 128], replicated, may hold values from 0 to 3
- measured: bfloat16 [2, 8, 18432], P('frame', 'row', 'depth'), may hold values from -6 to 6
- pixel_weight: int32 [2, 8, 18432], P('frame', 'row', 'depth'), may hold values 0 or 1
Outputs:
- camera: float32 [2, 8, 18432], P('frame', 'row', 'depth')
- residual: float32 [2, 8, 18432], P('frame', 'row', 'depth')
Inputs may be any that keep to these rules, and one draw needn't show every extreme that they name: `region_map`: the block that serves each lenslet.
All inputs are finite; a program needn't handle non-finite values. No bound on the sum of `pixel_weight` on one device may be relied on, other than what follows from the above.
Results may differ from a plain program's by a relative error of at most 0.0003.
Values may be sent and summed in bfloat16 or wider, within the bound.
A program may use at most 64 MiB of HBM per device.

v0:
```python
import jax
import jax.numpy as jnp
from jax import lax
from jax.sharding import PartitionSpec as P

PHASES = 144
BLOCKS = 4
TAP_SIDE = 5


def build_taps(planes, region_rows):
    tap_reach = TAP_SIDE // 2
    frames, row_count, merged = planes.shape
    col_count = merged // PHASES
    split_planes = planes.reshape(frames, row_count, col_count, PHASES)
    block_ids = jnp.arange(BLOCKS, dtype=jnp.int32)
    onehot = (region_rows[:, :, None] == block_ids[None, None, :]).astype(jnp.bfloat16)
    expanded = (split_planes[:, :, :, None, :] * onehot[None, :, :, :, None]).reshape(
        frames, row_count, col_count, BLOCKS * PHASES
    )
    return jnp.pad(expanded, ((0, 0), (0, 0), (tap_reach, tap_reach), (0, 0)))


def project(padded, spread_local, out_rows):
    tap_reach = TAP_SIDE // 2
    frames, ext_rows, ext_cols, _ = padded.shape
    col_count = ext_cols - 2 * tap_reach
    out_width = spread_local.shape[2]
    zero_start = jnp.zeros((frames * out_rows * col_count, out_width), jnp.float32)
    running = zero_start
    spread_slab = lax.all_gather(spread_local, "frame", axis=0, tiled=True)
    piece_rows = spread_slab.shape[0]
    flat_cols = padded.reshape(frames * ext_rows * ext_cols, piece_rows)
    for tap_row in range(TAP_SIDE):
        row_taps = spread_slab[:, tap_row * TAP_SIDE : (tap_row + 1) * TAP_SIDE, :].reshape(
            piece_rows, TAP_SIDE * out_width
        )
        product = jnp.dot(flat_cols, row_taps, preferred_element_type=jnp.float32)
        product = product.reshape(frames, ext_rows, ext_cols, TAP_SIDE, out_width)
        first_row = 2 * tap_reach - tap_row
        for tap_col in range(TAP_SIDE):
            first_col = 2 * tap_reach - tap_col
            shifted = product[
                :, first_row : first_row + out_rows, first_col : first_col + col_count, tap_col, :
            ]
            running = running + shifted.reshape(frames * out_rows * col_count, out_width)
    partial_value = running.reshape(frames, out_rows, col_count * out_width)
    return lax.psum_scatter(partial_value, "depth", scatter_dimension=2, tiled=True)


def body(volume, point_spread, region_map, measured, pixel_weight):
    tap_reach = TAP_SIDE // 2
    planes = volume[0]
    row_count = planes.shape[1]
    region_padded = jnp.pad(region_map, ((tap_reach, tap_reach), (0, 0)), constant_values=-1)
    all_rows = lax.all_gather(planes, "row", axis=1, tiled=True)
    extended = jnp.pad(all_rows, ((0, 0), (tap_reach, tap_reach), (0, 0)))
    padded = build_taps(extended, region_padded)
    piece_width = point_spread.shape[3]
    partial_value = project(padded, point_spread[0], all_rows.shape[1])
    frames, total_rows, merged = partial_value.shape
    split_partial = partial_value.reshape(frames, total_rows, merged // piece_width, piece_width)
    returned = lax.all_to_all(split_partial, "row", split_axis=1, concat_axis=3, tiled=True)
    camera = returned.reshape(frames, row_count, returned.shape[2] * returned.shape[3])
    residual = pixel_weight.astype(jnp.float32) * (camera - measured.astype(jnp.float32))
    return (camera, residual)


def solution(mesh):
    in_specs = (
        P("depth", "frame", "row", None),
        P("depth", "frame", None, "row"),
        P(),
        P("frame", "row", "depth"),
        P("frame", "row", "depth"),
    )
    out_specs = (P("frame", "row", "depth"), P("frame", "row", "depth"))
    return jax.shard_map(body, mesh=mesh, in_specs=in_specs, out_specs=out_specs, check_vma=False)
```

profile of v0, /device:TPU:0, one launch (start us, length us, event | category | flops | bytes accessed | tf_op | source)
XLA Modules:
  0.0 172.1 jit_solution(8674329077306728136)
XLA Ops:
  7.2 5.7 %copy.53 = bf16[1,288,25,36]{3,2,0,1:T(8,128)(2,1)S(1)} copy(bf16[1,288,25,36]{1,3,2,0:T(8,128)(2,1)} %param.6) | data formatting | bytes 1036800 | tf_op args[1]
  12.9 55.0 %all-gather.1 = bf16[1,576,25,36]{3,2,0,1:T(8,128)(2,1)S(1)} all-gather(bf16[1,288,25,36]{3,2,0,1:T(8,128)(2,1)S(1)} %copy.53), channel_id=3, replica_groups=mesh['frame'=2,'depth'=4,'row'=4] {'frame'}, dimensions={1}, use_global_device_ids=true | all-gather | bytes 1555200 | tf_op jit(solution)/shard_map/all_gather | solution.py:31
  67.9 2.8 %fusion.36 = (bf16[576,5,36]{2,1,0:T(8,128)(2,1)S(1)}, bf16[576,5,36]{2,1,0:T(8,128)(2,1)S(1)}, bf16[576,5,36]{2,1,0:T(8,128)(2,1)}, bf16[576,5,36]{2,1,0:T(8,128)(2,1)}, bf16[576,5,36]{2,1,0:T(8,128)(2,1)}) fusion(bf16[576,25,36]{2,1,0:T(8,128)(2,1)S(1)} %bitcast.93), kind=kLoop, calls=%fused_computation.47 | loop fusion | bytes 2073600 | tf_op jit(solution)/shard_map/slice | solution.py:35
  71.8 7.9 %all-gather = bf16[1,1,8,18432]{3,1,0,2:T(2,128)(2,1)S(1)} all-gather(bf16[1,1,2,18432]{3,1,0,2:T(2,128)(2,1)S(1)} %copy.50), channel_id=2, replica_groups=mesh['frame'=2,'depth'=4,'row'=4] {'row'}, dimensions={2}, use_global_device_ids=true | all-gather | bytes 368640 | tf_op jit(solution)/shard_map/all_gather | solution.py:56
  80.0 1.4 mul.30
  83.0 2.7 %copy.52 = bf16[1,12,128,576]{3,2,1,0:T(8,128)(2,1)S(1)} copy(bf16[1,12,128,576]{2,3,1,0:T(8,128)(2,1)} %bitcast.94) | data formatting | bytes 3538944 | tf_op jit(solution)/shard_map/mul | solution.py:18
  87.9 1.9 %copy.67 = f32[1,8,128,1,36]{4,2,1,3,0:T(8,128)} copy(f32[1,8,128,1,36]{2,4,3,1,0:T(8,128)} %get-tuple-element.11) | data formatting | bytes 294912 | tf_op jit(solution)/shard_map/slice | solution.py:43
  89.8 2.0 %reshape_squeeze.84 = f32[1,8,4608]{2,1,0:T(8,128)} reshape(f32[1,8,128,1,36]{4,2,1,3,0:T(8,128)} %copy.67) | data formatting | bytes 294912 | tf_op jit(solution)/shard_map/reshape;squeeze | solution.py:46
  91.8 1.9 %copy.66 = f32[1,8,128,1,36]{4,2,1,3,0:T(8,128)} copy(f32[1,8,128,1,36]{2,4,3,1,0:T(8,128)} %get-tuple-element.12) | data formatting | bytes 294912 | tf_op jit(solution)/shard_map/slice | solution.py:43
  93.7 2.0 %reshape_squeeze.83 = f32[1,8,4608]{2,1,0:T(8,128)} reshape(f32[1,8,128,1,36]{4,2,1,3,0:T(8,128)} %copy.66) | data formatting | bytes 294912 | tf_op jit(solution)/shard_map/reshape;squeeze | solution.py:46
  95.7 1.9 %copy.65 = f32[1,8,128,1,36]{4,2,1,3,0:T(8,128)} copy(f32[1,8,128,1,36]{2,4,3,1,0:T(8,128)} %get-tuple-element.13) | data formatting | bytes 294912 | tf_op jit(solution)/shard_map/slice | solution.py:43
  97.6 2.0 %reshape_squeeze.82 = f32[1,8,4608]{2,1,0:T(8,128)} reshape(f32[1,8,128,1,36]{4,2,1,3,0:T(8,128)} %copy.65) | data formatting | bytes 294912 | tf_op jit(solution)/shard_map/reshape;squeeze | solution.py:46
  100.6 2.0 %reshape_squeeze.81 = f32[1,8,4608]{2,1,0:T(8,128)} reshape(f32[1,8,128,1,36]{4,2,1,3,0:T(8,128)} %copy.64) | data formatting | bytes 294912 | tf_op jit(solution)/shard_map/reshape;squeeze | solution.py:46
  103.7 2.0 %reshape_squeeze.80 = f32[1,8,4608]{2,1,0:T(8,128)} reshape(f32[1,8,128,1,36]{4,2,1,3,0:T(8,128)} %copy.63) | data formatting | bytes 294912 | tf_op jit(solution)/shard_map/reshape;squeeze | solution.py:46
  105.6 1.8 %reshape.379 = bf16[576,180]{1,0:T(8,128)(2,1)S(1)} reshape(bf16[576,5,36]{2,1,0:T(8,128)(2,1)} %get-tuple-element.4) | data formatting | bytes 414720 | tf_op jit(solution)/shard_map/reshape | solution.py:35
  110.5 1.4 copy-done
  113.0 2.0 %reshape_squeeze.79 = f32[1,8,4608]{2,1,0:T(8,128)} reshape(f32[1,8,128,1,36]{4,2,1,3,0:T(8,128)} %copy.61) | data formatting | bytes 294912 | tf_op jit(solution)/shard_map/reshape;squeeze | solution.py:46
  115.0 1.8 %reshape.377 = bf16[576,180]{1,0:T(8,128)(2,1)S(1)} reshape(bf16[576,5,36]{2,1,0:T(8,128)(2,1)} %get-tuple-element.5) | data formatting | bytes 414720 | tf_op jit(solution)/shard_map/reshape | solution.py:35
  118.7 2.6 %fusion.16 = f32[1,12,132,5,36]{2,4,3,1,0:T(8,128)} fusion(bf16[5,36,576,1]{2,1,0,3:T(8,128)(2,1)S(1)} %reshape.370, bf16[1,12,128,576]{3,2,1,0:T(8,128)(2,1)S(1)} %copy.52), kind=kOutput, calls=%fused_computation.12 | convolution fusion | flops 328458240 | bytes 3117312 | tf_op jit(solution)/shard_map/dot_general | solution.py:38
  121.3 2.1 %reshape.375 = bf16[576,180]{1,0:T(8,128)(2,1)S(1)} reshape(bf16[576,5,36]{2,1,0:T(8,128)(2,1)} %get-tuple-element.6) | data formatting | bytes 414720 | tf_op jit(solution)/shard_map/reshape | solution.py:35
  125.2 2.6 %fusion.13 = f32[1,12,132,5,36]{2,4,3,1,0:T(8,128)} fusion(bf16[5,36,576,1]{2,1,0,3:T(8,128)(2,1)S(1)} %reshape.369, bf16[1,12,128,576]{3,2,1,0:T(8,128)(2,1)S(1)} %copy.52), kind=kOutput, calls=%fused_computation.11 | convolution fusion | flops 328458240 | bytes 3117312 | tf_op jit(solution)/shard_map/dot_general | solution.py:38
  129.8 2.9 %fusion.37 = (f32[1,8,128,1,36]{2,4,3,1,0:T(8,128)S(1)}, f32[1,8,128,1,36]{2,4,3,1,0:T(8,128)S(1)}, f32[1,8,128,1,36]{2,4,3,1,0:T(8,128)S(1)}) fusion(f32[1,12,132,5,36]{2,4,3,1,0:T(8,128)} %copy-done, f32[1,12,132,5,36]{2,4,3,1,0:T(8,128)} %fusion.16, f32[1,12,132,5,36]{2,4,3,1,0:T(8,128)} %fusion.13, f32[1,12,132,5,36]{2,4,3,1,0:T(8,128)S(1)} %fusion.10), kind=kLoop, calls=%fused_computation.48 | loop fusion | flops 589824 | bytes 3244032 | tf_op jit(solution)/shard_map/slice | solution.py:43
  135.2 20.1 %reduce-scatter.2.cloned.1.call-done = f32[1,8,1152]{2,1,0:T(8,128)} async-done(((f32[1,8,4608]{2,1,0:T(8,128)}), f32[1,8,1152]{2,1,0:T(8,128)}) %reduce-scatter.2.cloned.1.call-update) | async-done | bytes 36880 | tf_op jit(solution)/shard_map/reduce_scatter | solution.py:48
  156.3 6.5 %all_to_all.15 = f32[4,1,2304]{2,1,0:T(1,128)S(1)} all-to-all(f32[4,1,2304]{2,1,0:T(1,128)S(1)} %reshape.383), channel_id=1, replica_groups=mesh['frame'=2,'depth'=4,'row'=4] {'row'}, dimensions={0} | all-to-all | bytes 73728 | tf_op jit(solution)/shard_map/all_to_all | solution.py:63
  (68 shorter events, 22.5 us)
Async XLA Ops:
  7.2 148.0 %reduce-scatter.2.cloned.1.call-start = ((), (), s32[]{:S(2)}) async-start(), calls=%async_computation.2 | async-start | bytes 184320 | tf_op jit(solution)/shard_map/reduce_scatter | solution.py:48
  70.8 0.8 copy-start.11
  70.8 0.9 copy-start.8
  110.5 1.5 copy-start
  132.7 1.6 copy-start.1
  132.8 1.6 copy-start.2
  132.8 1.6 copy-start.3
  132.8 1.6 copy-start.4
  132.8 1.6 copy-start.5
  132.8 1.6 copy-start.6
  133.8 30.7 %copy-start.9 = (s32[1,2,4608]{2,1,0:T(2,128)S(1)}, s32[1,2,4608]{2,1,0:T(2,128)}, u32[]{:S(2)}) copy-start(s32[1,2,4608]{2,1,0:T(2,128)} %param.9) | copy-start | bytes 110596
  133.8 30.7 %copy-start.10 = (bf16[1,2,4608]{2,1,0:T(2,128)(2,1)S(1)}, bf16[1,2,4608]{2,1,0:T(2,128)(2,1)}, u32[]{:S(2)}) copy-start(bf16[1,2,4608]{2,1,0:T(2,128)(2,1)} %param.8) | copy-start | bytes 55300
  164.6 0.7 copy-start.7
Sparse Core Ops, SparseCore 0:
  135.3 19.8 reduce-scatter.1
where the time goes:
time: 173 us; the launch traced here: 172 us
  blocking collectives  69.4 us (40%)
  local copies, waits for them, and re-layouts  53.1 us (31%)
  waiting for transfers between devices  20.1 us (12%)
  between operations  14.4 us (8%)
  matrix products  8.66 us (5%)
  other arithmetic  6.41 us (4%)
    all_gather x1, blocking collectives, project(): spread_slab = lax.all_gather(spread_local, 'frame', axis=0, tiled=True)  55 us
    reduce_scatter x1, waiting for transfers between devices, project(): lax.psum_scatter(partial_value, 'depth', scatter_dimension=2, tiled=True)  20.1 us
    another operation x8, local copies, waits for them, and re-layouts, project(): shifted.reshape(frames * out_rows * col_count, out_width)  12.5 us
    slice x10, local copies, waits for them, and re-layouts, project(): product[:, first_row:first_row + out_rows, first_col:first_col + col_coun...  10.3 us
    reshape x10, local copies, waits for them, and re-layouts, project(): spread_slab[:, tap_row * TAP_SIDE:(tap_row + 1) * TAP_SIDE, :]  9.78 us
    dot_general x5, matrix products, project(): product = jnp.dot(flat_cols, row_taps, preferred_element_type=jnp.float32)  8.66 us
    unnamed x30, local copies, waits for them, and re-layouts  7.89 us
    all_gather x1, blocking collectives, body(): all_rows = lax.all_gather(planes, 'row', axis=1, tiled=True)  7.85 us
  transfers between devices with their start and end apart: 1, of which 1 were waited for; matrix products, arithmetic and copies ran while one was open for 0% of the time, Pallas kernels for 0%

commit v1 on v0

--- a/solution.py
+++ b/solution.py
@@ -1,6 +1,10 @@
+import functools
+
 import jax
 import jax.numpy as jnp
 from jax import lax
+from jax.experimental import pallas as pl
+from jax.experimental.pallas import tpu as pltpu
 from jax.sharding import PartitionSpec as P
 
 PHASES = 144
@@ -48,7 +52,7 @@
     return lax.psum_scatter(partial_value, "depth", scatter_dimension=2, tiled=True)
 
 
-def body(volume, point_spread, region_map, measured, pixel_weight):
+def plain_body(volume, point_spread, region_map, measured, pixel_weight):
     tap_reach = TAP_SIDE // 2
     planes = volume[0]
     row_count = planes.shape[1]
@@ -66,6 +70,200 @@
     return (camera, residual)
 
 
+def round_up(value, step):
+    return (value + step - 1) // step * step
+
+
+def remote(src, dst, send_sem, recv_sem, device):
+    return pltpu.make_async_remote_copy(
+        src_ref=src, dst_ref=dst, send_sem=send_sem, recv_sem=recv_sem,
+        device_id=device, device_id_type=pl.DeviceIdType.MESH,
+    )
+
+
+def kernel(frames, depths, row_shards, vin, w_hbm, region, cam, vol, wraw, wflat, xmask, part, xrecv, zsend,
+           zrecv, yred, fin, w_sem, g_send, g_recv, x_send, x_recv, z_send, z_recv, y_send, y_recv):
+    reach = TAP_SIDE // 2
+    rows_here, phases, cols = vin.shape
+    rows = rows_here * row_shards
+    taps, width, depth_rows = w_hbm.shape
+    blocks_here = depth_rows // phases
+    stride = wflat.shape[0] // TAP_SIDE
+    qpad = part.shape[3]
+    col_share = cols // depths
+    quads = rows // depths
+    me_f, me_d, me_r = lax.axis_index("frame"), lax.axis_index("depth"), lax.axis_index("row")
+    other_f = 1 - me_f
+    core_r = me_r + 1 - 2 * lax.rem(me_r, 2)
+    far_r = lax.rem(me_r + 2, row_shards)
+    far_core_r = far_r + 1 - 2 * lax.rem(far_r, 2)
+
+    w_copy = pltpu.make_async_copy(w_hbm, wraw, w_sem)
+    w_copy.start()
+
+    x_dev = (other_f, me_d, me_r)
+    core_dev = (me_f, me_d, core_r)
+    far_dev = (me_f, me_d, far_r)
+    diag_dev = (other_f, me_d, far_r)
+    partners = [x_dev, diag_dev]
+    partners += [(me_f, me_d, lax.rem(me_r + step, row_shards)) for step in range(1, row_shards)]
+    partners += [(me_f, lax.rem(me_d + step, depths), me_r) for step in range(1, depths)]
+    barrier = pltpu.get_barrier_semaphore()
+    for device in partners:
+        pl.semaphore_signal(barrier, inc=1, device_id=device, device_id_type=pl.DeviceIdType.MESH)
+    pl.semaphore_wait(barrier, len(partners))
+
+    def slot(frame, row):
+        return vol.at[frame, pl.ds(row * rows_here, rows_here)]
+
+    def gather(index, src, frame, row, device):
+        return remote(src, slot(frame, row), g_send.at[index], g_recv.at[index], device)
+
+    own_x = gather(0, vin, me_f, me_r, x_dev)
+    own_far = gather(1, vin, me_f, me_r, far_dev)
+    own_diag = gather(2, vin, me_f, me_r, diag_dev)
+    own_core = gather(3, vin, me_f, me_r, core_dev)
+    for copy in (own_x, own_far, own_diag, own_core):
+        copy.start()
+    slot(me_f, me_r)[...] = vin[...]
+
+    w_copy.wait()
+    for tap_col in range(TAP_SIDE):
+        pieces = [wraw[(TAP_SIDE - 1 - at) * TAP_SIDE + tap_col] for at in range(TAP_SIDE)]
+        wflat[tap_col * stride:tap_col * stride + width, :] = jnp.concatenate(pieces, axis=1)
+    edge = jnp.zeros((reach * depth_rows, frames * cols), jnp.bfloat16)
+    xmask[:reach * depth_rows, :] = edge
+    xmask[(rows + reach) * depth_rows:, :] = edge
+
+    own_x.wait_recv()
+    fwd_x = gather(4, slot(other_f, me_r), other_f, me_r, core_dev)
+    fwd_x.start()
+    own_far.wait_recv()
+    fwd_far = gather(5, slot(me_f, far_r), me_f, far_r, core_dev)
+    fwd_far.start()
+    own_diag.wait_recv()
+    fwd_diag = gather(6, slot(other_f, far_r), other_f, far_r, core_dev)
+    fwd_diag.start()
+    for copy in (own_core, fwd_x, fwd_far, fwd_diag):
+        copy.wait_recv()
+
+    first_block = me_f * blocks_here
+    for row in range(rows):
+        for block in range(blocks_here):
+            keep = (region[row:row + 1, :] == first_block + block).astype(jnp.float32).astype(jnp.bfloat16)
+            top = (row + reach) * depth_rows + block * phases
+            for frame in range(frames):
+                xmask[top:top + phases, frame * cols:(frame + 1) * cols] = vol[frame, row] * keep
+
+    lane = lax.broadcasted_iota(jnp.int32, (qpad, cols), 1)
+    x_copies = []
+    for quad in range(quads):
+        sums = [[None] * frames for _ in range(depths)]
+        for at in range(depths):
+            row = quad * depths + at
+            slab = xmask[row * depth_rows:(row + TAP_SIDE) * depth_rows, :]
+            product = jnp.dot(wflat[...], slab, preferred_element_type=jnp.float32)
+            for frame in range(frames):
+                total = None
+                for tap_col in range(TAP_SIDE):
+                    shift = tap_col - reach
+                    piece = product[tap_col * stride:tap_col * stride + qpad, frame * cols:(frame + 1) * cols]
+                    if shift:
+                        piece = pltpu.roll(piece, shift % cols, 1)
+                        inside = lane >= shift if shift > 0 else lane < cols + shift
+                        piece = jnp.where(inside, piece, 0.0)
+                    total = piece if total is None else total + piece
+                sums[at][frame] = total
+        for frame in range(frames):
+            for share in range(depths):
+                packed = None
+                for at in range(depths):
+                    shift = (at - share) * col_share % cols
+                    moved = pltpu.roll(sums[at][frame], shift, 1) if shift else sums[at][frame]
+                    packed = moved if packed is None else jnp.where(lane >= at * col_share, moved, packed)
+                part[frame, quad, share] = packed
+        copy = remote(part.at[other_f, quad], xrecv.at[quad], x_send.at[quad], x_recv.at[quad], x_dev)
+        copy.start()
+        x_copies.append(copy)
+
+    z_copies = []
+    for quad in range(quads):
+        x_copies[quad].wait_recv()
+        for share in range(depths):
+            zsend[quad, share] = part[me_f, quad, share] + xrecv[quad, share]
+        for step in range(1, depths):
+            to = lax.rem(me_d + step, depths)
+            copy = remote(zsend.at[quad, to], zrecv.at[quad, step - 1], z_send.at[quad, step - 1],
+                          z_recv.at[quad, step - 1], (me_f, to, me_r))
+            copy.start()
+            z_copies.append(copy)
+    for quad in range(quads):
+        total = zsend[quad, me_d]
+        for step in range(1, depths):
+            z_copies[quad * (depths - 1) + step - 1].wait_recv()
+            total = total + zrecv[quad, step - 1]
+        yred[quad] = total
+
+    shares = row_shards // quads
+    y_copies = []
+    for step in range(1, row_shards):
+        to = lax.rem(me_r + step, row_shards)
+        copy = remote(yred.at[to // shares], fin.at[me_r], y_send.at[step - 1], y_recv.at[step - 1], (me_f, me_d, to))
+        copy.start()
+        y_copies.append(copy)
+    fin[me_r] = yred[me_r // shares]
+    for copy in y_copies:
+        copy.wait_recv()
+    lanes_here = rows_here * col_share
+    back = lax.rem(cols - lax.rem(me_r, shares) * lanes_here, cols)
+    for source in range(row_shards):
+        mine = pltpu.roll(fin[source], back, 1)
+        cam[:, source * width:(source + 1) * width] = mine.T[:lanes_here, :width]
+    for copy in (own_x, own_far, own_diag, own_core, fwd_x, fwd_far, fwd_diag, *x_copies, *z_copies, *y_copies):
+        copy.wait_send()
+
+
+def fused_body(sizes, volume, point_spread, region_map, measured, pixel_weight):
+    frames, depths, row_shards = sizes
+    _, _, rows_here, merged = volume.shape
+    cols = merged // PHASES
+    _, depth_rows, taps, width = point_spread.shape
+    rows = rows_here * row_shards
+    quads = rows // depths
+    qpad = round_up(width, 8)
+    stride = round_up(width, 16)
+    vin = volume.reshape(rows_here, cols, PHASES).transpose(0, 2, 1)
+    spread = point_spread.reshape(depth_rows, taps, width).transpose(1, 2, 0)
+    col_share = cols // depths
+    vmem = pl.BlockSpec(memory_space=pltpu.VMEM)
+    dma = pltpu.SemaphoreType.DMA
+    cam = pl.pallas_call(
+        functools.partial(kernel, frames, depths, row_shards),
+        out_shape=jax.ShapeDtypeStruct((rows_here * col_share, row_shards * width), jnp.float32),
+        in_specs=[vmem, pl.BlockSpec(memory_space=pl.ANY), vmem],
+        out_specs=vmem,
+        scratch_shapes=[
+            pltpu.VMEM((frames, rows, PHASES, cols), jnp.bfloat16),
+            pltpu.VMEM((taps, width, depth_rows), jnp.bfloat16),
+            pltpu.VMEM((TAP_SIDE * stride, TAP_SIDE * depth_rows), jnp.bfloat16),
+            pltpu.VMEM(((rows + TAP_SIDE - 1) * depth_rows, frames * cols), jnp.bfloat16),
+            pltpu.VMEM((frames, quads, depths, qpad, cols), jnp.float32),
+            pltpu.VMEM((quads, depths, qpad, cols), jnp.float32),
+            pltpu.VMEM((quads, depths, qpad, cols), jnp.float32),
+            pltpu.VMEM((quads, depths - 1, qpad, cols), jnp.float32),
+            pltpu.VMEM((quads, qpad, cols), jnp.float32),
+            pltpu.VMEM((row_shards, qpad, cols), jnp.float32),
+            dma, dma((7,)), dma((7,)), dma((quads,)), dma((quads,)),
+            dma((quads, depths - 1)), dma((quads, depths - 1)),
+            dma((row_shards - 1,)), dma((row_shards - 1,)),
+        ],
+        compiler_params=pltpu.CompilerParams(collective_id=0, has_side_effects=True),
+    )(vin, spread, region_map)
+    camera = cam.reshape(measured.shape)
+    residual = pixel_weight.astype(jnp.float32) * (camera - measured.astype(jnp.float32))
+    return (camera, residual)
+
+
 def solution(mesh):
     in_specs = (
         P("depth", "frame", "row", None),
@@ -75,4 +273,15 @@
         P("frame", "row", "depth"),
     )
     out_specs = (P("frame", "row", "depth"), P("frame", "row", "depth"))
+    sizes = (mesh.shape["frame"], mesh.shape["depth"], mesh.shape["row"])
+
+    def body(volume, *rest):
+        rows = volume.shape[2] * sizes[2]
+        blocks_fit = rest[0].shape[1] % PHASES == 0
+        quads = rows // sizes[1] if rows % sizes[1] == 0 else 0
+        packs = quads and sizes[2] % quads == 0 and (volume.shape[3] // PHASES) == 128
+        if sizes[0] == 2 and sizes[2] == 4 and volume.shape[1] == 1 and blocks_fit and packs:
+            return fused_body(sizes, volume, *rest)
+        return plain_body(volume, *rest)
+
     return jax.shard_map(body, mesh=mesh, in_specs=in_specs, out_specs=out_specs, check_vma=False)

time: 173 us -> 30.6 us (0.18)
  blocking collectives: 69.4 us -> 0 us
  local copies, waits for them, and re-layouts: 53.1 us -> 2.8 us
  Pallas kernels: 0 us -> 26.2 us
  waiting for transfers between devices: 20.1 us -> 0 us
  between operations: 14.4 us -> 0.69 us
  matrix products: 8.66 us -> 0 us
  other arithmetic: 6.41 us -> 0.65 us
    all_gather x2 -> x0, blocking collectives: 62.9 us -> none  [the longest x1 55 us: project(): spread_slab = lax.all_gather(spread_local, 'frame', axis=0, tiled=True)]
    pallas_call x0 -> x1, Pallas kernels: none -> 26.2 us  [fused_body(): pl.pallas_call(functools.partial(kernel, frames, depths, row_shards), out...]
    reduce_scatter x1 -> x0, waiting for transfers between devices: 20.1 us -> none  [project(): lax.psum_scatter(partial_value, 'depth', scatter_dimension=2, tiled=True)]
    slice x11 -> x0, local copies, waits for them, and re-layouts: 13.1 us -> none  [the longest x10 10.3 us: project(): product[:, first_row:first_row + out_rows, first_col:first_col + col_coun...]
    another operation x8 -> x0, local copies, waits for them, and re-layouts: 12.5 us -> none  [project(): shifted.reshape(frames * out_rows * col_count, out_width)]
    dot_general x5 -> x0, matrix products: 8.66 us -> none  [project(): product = jnp.dot(flat_cols, row_taps, preferred_element_type=jnp.float32)]
    reshape x12 -> x3, local copies, waits for them, and re-layouts: 10.9 us -> 2.78 us  [the longest x2 1.82 us: fused_body(): vin = volume.reshape(rows_here, cols, PHASES).transpose(0, 2, 1)]
    unnamed x30 -> x6, local copies, waits for them, and re-layouts: 7.89 us -> 0.02 us
  transfers between devices with their start and end apart: 1 -> 0, of which waited for: 1 -> 0; matrix products, arithmetic and copies ran while one was open for 0% -> 0% of each run, Pallas kernels for 0% -> 0%
where the time goes in v1:
time: 30.6 us; the launch traced here: 30.3 us
  Pallas kernels  26.2 us (86%)
  local copies, waits for them, and re-layouts  2.8 us (9%)
  between operations  0.69 us (2%)
  other arithmetic  0.65 us (2%)
    pallas_call x1, Pallas kernels, fused_body(): pl.pallas_call(functools.partial(kernel, frames, depths, row_shards), out...  26.2 us
    reshape x2, local copies, waits for them, and re-layouts, fused_body(): vin = volume.reshape(rows_here, cols, PHASES).transpose(0, 2, 1)  1.82 us
    reshape x1, local copies, waits for them, and re-layouts, fused_body(): camera = cam.reshape(measured.shape)  0.97 us
    mul x1, other arithmetic, fused_body(): pixel_weight.astype(jnp.float32) * (camera - measured.astype(jnp.float32))  0.65 us

profile of v1, /device:TPU:0, one launch (start us, length us, event | category | flops | bytes accessed | tf_op | source)
XLA Modules:
  0.0 30.3 jit_solution(14023557326361149068)
XLA Ops:
  0.6 1.1 %reshape.13 = bf16[2,128,144]{2,1,0:T(8,128)(2,1)S(1)} reshape(bf16[1,1,2,18432]{3,2,1,0:T(2,128)(2,1)} %param.5) | data formatting | bytes 147456 | tf_op jit(solution)/shard_map/reshape | solution.py:235
  1.7 0.7 %copy.7 = bf16[2,128,144]{1,2,0:T(8,128)(2,1)} copy(bf16[2,128,144]{2,1,0:T(8,128)(2,1)S(1)} %reshape.13) | data formatting | bytes 147456 | tf_op jit(solution)/shard_map/reshape | solution.py:235
  2.5 26.2 %shard_map.68 = f32[64,144]{1,0:T(8,128)} custom-call(bf16[2,144,128]{2,1,0:T(8,128)(2,1)} %bitcast.5, bf16[25,36,288]{2,1,0:T(8,128)(2,1)} %bitcast.4, s32[8,128]{1,0:T(8,128)} %region.1), custom_call_target="tpu_custom_call" | custom-call | tf_op jit(solution)/shard_map/pallas_call | solution.py:240
  28.7 0.0 copy-start.1
  28.7 0.0 copy-start.2
  28.7 1.0 %reshape.15 = f32[1,2,4608]{2,1,0:T(2,128)S(1)} reshape(f32[64,144]{1,0:T(8,128)} %shard_map.68) | data formatting | bytes 73728 | tf_op jit(solution)/shard_map/reshape | solution.py:262
  29.6 0.0 copy-done.1
  29.7 0.0 copy-done.2
  29.7 0.0 copy-start
  29.7 0.6 %subtract_multiply_fusion = f32[1,2,4608]{2,1,0:T(2,128)} fusion(f32[1,2,4608]{2,1,0:T(2,128)S(1)} %reshape.15, bf16[1,2,4608]{2,1,0:T(2,128)(2,1)S(1)} %copy-done.2, s32[1,2,4608]{2,1,0:T(2,128)S(1)} %copy-done.1), kind=kLoop, calls=%fused_computation | loop fusion | flops 36864 | bytes 129024 | tf_op jit(solution)/shard_map/mul | solution.py:263
  30.3 0.0 copy-done
Async XLA Ops:
  28.7 1.0 %copy-start.1 = (s32[1,2,4608]{2,1,0:T(2,128)S(1)}, s32[1,2,4608]{2,1,0:T(2,128)}, u32[]{:S(2)}) copy-start(s32[1,2,4608]{2,1,0:T(2,128)} %param.9) | copy-start | bytes 110596
  28.7 1.0 %copy-start.2 = (bf16[1,2,4608]{2,1,0:T(2,128)(2,1)S(1)}, bf16[1,2,4608]{2,1,0:T(2,128)(2,1)}, u32[]{:S(2)}) copy-start(bf16[1,2,4608]{2,1,0:T(2,128)(2,1)} %param.8) | copy-start | bytes 55300
  29.7 0.7 %copy-start = (f32[1,2,4608]{2,1,0:T(2,128)}, f32[1,2,4608]{2,1,0:T(2,128)S(1)}, u32[]{:S(2)}) copy-start(f32[1,2,4608]{2,1,0:T(2,128)S(1)} %reshape.15) | copy-start | bytes 110596

commit v2 on v1

--- a/solution.py
+++ b/solution.py
@@ -1,4 +1,5 @@
 import functools
+import math
 
 import jax
 import jax.numpy as jnp
@@ -81,7 +82,29 @@
     )
 
 
-def kernel(frames, depths, row_shards, vin, w_hbm, region, cam, vol, wraw, wflat, xmask, part, xrecv, zsend,
+def lanes_from_rows(raw, wide, pieces, vin):
+    rows_here, phases, cols = vin.shape
+    group = math.lcm(phases, 128) // phases
+    span = group * phases
+    groups = cols // group
+    wide[:, span:] = jnp.zeros((wide.shape[0], wide.shape[1] - span), jnp.float32)
+    for at in range(groups):
+        strip = raw[:, at * span:(at + 1) * span].astype(jnp.float32)
+        for row in range(rows_here):
+            wide[row * groups + at:row * groups + at + 1, :span] = strip[row:row + 1]
+    for member in range(group):
+        for half in range(pieces.shape[0]):
+            first = member * phases + half * 128
+            pieces[half, pl.ds(member, rows_here * groups, stride=group), :] = wide[:, first:first + 128]
+    for row in range(rows_here):
+        for half in range(pieces.shape[0]):
+            count = min(128, phases - half * 128)
+            turned = pieces[half, row * cols:(row + 1) * cols, :].T
+            vin[row, half * 128:half * 128 + count, :] = turned[:count].astype(jnp.bfloat16)
+
+
+def kernel(frames, depths, row_shards, v_hbm, w_hbm, region, m_hbm, p_hbm, cam, res, raw, wide, pieces, vin,
+           mraw, praw, in_sem, vol, wraw, wflat, xmask, part, xrecv, zsend,
            zrecv, yred, fin, w_sem, g_send, g_recv, x_send, x_recv, z_send, z_recv, y_send, y_recv):
     reach = TAP_SIDE // 2
     rows_here, phases, cols = vin.shape
@@ -98,8 +121,6 @@
     far_r = lax.rem(me_r + 2, row_shards)
     far_core_r = far_r + 1 - 2 * lax.rem(far_r, 2)
 
-    w_copy = pltpu.make_async_copy(w_hbm, wraw, w_sem)
-    w_copy.start()
 
     x_dev = (other_f, me_d, me_r)
     core_dev = (me_f, me_d, core_r)
@@ -111,6 +132,16 @@
     barrier = pltpu.get_barrier_semaphore()
     for device in partners:
         pl.semaphore_signal(barrier, inc=1, device_id=device, device_id_type=pl.DeviceIdType.MESH)
+    v_copy = pltpu.make_async_copy(v_hbm, raw, in_sem.at[0])
+    v_copy.start()
+    w_copy = pltpu.make_async_copy(w_hbm, wraw, w_sem)
+    w_copy.start()
+    m_copy = pltpu.make_async_copy(m_hbm, mraw, in_sem.at[1])
+    m_copy.start()
+    p_copy = pltpu.make_async_copy(p_hbm, praw, in_sem.at[2])
+    p_copy.start()
+    v_copy.wait()
+    lanes_from_rows(raw, wide, pieces, vin)
     pl.semaphore_wait(barrier, len(partners))
 
     def slot(frame, row):
@@ -129,8 +160,8 @@
 
     w_copy.wait()
     for tap_col in range(TAP_SIDE):
-        pieces = [wraw[(TAP_SIDE - 1 - at) * TAP_SIDE + tap_col] for at in range(TAP_SIDE)]
-        wflat[tap_col * stride:tap_col * stride + width, :] = jnp.concatenate(pieces, axis=1)
+        bands = [wraw[(TAP_SIDE - 1 - at) * TAP_SIDE + tap_col] for at in range(TAP_SIDE)]
+        wflat[tap_col * stride:tap_col * stride + width, :] = jnp.concatenate(bands, axis=1)
     edge = jnp.zeros((reach * depth_rows, frames * cols), jnp.bfloat16)
     xmask[:reach * depth_rows, :] = edge
     xmask[(rows + reach) * depth_rows:, :] = edge
@@ -216,9 +247,29 @@
         copy.wait_recv()
     lanes_here = rows_here * col_share
     back = lax.rem(cols - lax.rem(me_r, shares) * lanes_here, cols)
-    for source in range(row_shards):
-        mine = pltpu.roll(fin[source], back, 1)
-        cam[:, source * width:(source + 1) * width] = mine.T[:lanes_here, :width]
+    turned = jnp.concatenate(
+        [pltpu.roll(fin[source], back, 1).T[:lanes_here, :width] for source in range(row_shards)], axis=1
+    )
+    halves = pieces.shape[0]
+    for half in range(halves):
+        count = min(128, phases - half * 128)
+        pieces[half, :lanes_here, :count] = turned[:, half * 128:half * 128 + count]
+    group = math.lcm(phases, 128) // phases
+    span = group * phases
+    per_row = col_share // group
+    members = []
+    for member in range(group):
+        for half in range(halves):
+            count = min(128, phases - half * 128)
+            members.append(pieces[half, pl.ds(member, rows_here * per_row, stride=group), :][:, :count])
+    strips = jnp.concatenate(members, axis=1)
+    for row in range(rows_here):
+        for at in range(per_row):
+            line = row * per_row + at
+            cam[row:row + 1, at * span:(at + 1) * span] = strips[line:line + 1]
+    m_copy.wait()
+    p_copy.wait()
+    res[...] = praw[...].astype(jnp.float32) * (cam[...] - mraw[...].astype(jnp.float32))
     for copy in (own_x, own_far, own_diag, own_core, fwd_x, fwd_far, fwd_diag, *x_copies, *z_copies, *y_copies):
         copy.wait_send()
 
@@ -232,17 +283,26 @@
     quads = rows // depths
     qpad = round_up(width, 8)
     stride = round_up(width, 16)
-    vin = volume.reshape(rows_here, cols, PHASES).transpose(0, 2, 1)
+    group = math.lcm(PHASES, 128) // PHASES
+    span = group * PHASES
+    image = (rows_here, cols // depths * PHASES)
     spread = point_spread.reshape(depth_rows, taps, width).transpose(1, 2, 0)
-    col_share = cols // depths
     vmem = pl.BlockSpec(memory_space=pltpu.VMEM)
+    hbm = pl.BlockSpec(memory_space=pl.ANY)
     dma = pltpu.SemaphoreType.DMA
-    cam = pl.pallas_call(
+    camera, residual = pl.pallas_call(
         functools.partial(kernel, frames, depths, row_shards),
-        out_shape=jax.ShapeDtypeStruct((rows_here * col_share, row_shards * width), jnp.float32),
-        in_specs=[vmem, pl.BlockSpec(memory_space=pl.ANY), vmem],
-        out_specs=vmem,
+        out_shape=[jax.ShapeDtypeStruct(image, jnp.float32)] * 2,
+        in_specs=[hbm, hbm, vmem, hbm, hbm],
+        out_specs=[vmem, vmem],
         scratch_shapes=[
+            pltpu.VMEM((rows_here, merged), jnp.bfloat16),
+            pltpu.VMEM((rows_here * cols // group, span + 128), jnp.float32),
+            pltpu.VMEM((round_up(PHASES, 128) // 128, rows_here * cols, 128), jnp.float32),
+            pltpu.VMEM((rows_here, PHASES, cols), jnp.bfloat16),
+            pltpu.VMEM(image, jnp.bfloat16),
+            pltpu.VMEM(image, jnp.int32),
+            dma((3,)),
             pltpu.VMEM((frames, rows, PHASES, cols), jnp.bfloat16),
             pltpu.VMEM((taps, width, depth_rows), jnp.bfloat16),
             pltpu.VMEM((TAP_SIDE * stride, TAP_SIDE * depth_rows), jnp.bfloat16),
@@ -258,10 +318,8 @@
             dma((row_shards - 1,)), dma((row_shards - 1,)),
         ],
         compiler_params=pltpu.CompilerParams(collective_id=0, has_side_effects=True),
-    )(vin, spread, region_map)
-    camera = cam.reshape(measured.shape)
-    residual = pixel_weight.astype(jnp.float32) * (camera - measured.astype(jnp.float32))
-    return (camera, residual)
+    )(volume.reshape(rows_here, merged), spread, region_map, measured.reshape(image), pixel_weight.reshape(image))
+    return (camera.reshape(measured.shape), residual.reshape(measured.shape))
 
 
 def solution(mesh):

time: 30.6 us -> 29.1 us (0.951)
  local copies, waits for them, and re-layouts: 2.8 us -> 2.01 us
  other arithmetic: 0.65 us -> 0 us
    reshape x3 -> x0, local copies, waits for them, and re-layouts: 2.78 us -> none  [the longest x2 1.82 us: fused_body(): vin = volume.reshape(rows_here, cols, PHASES).transpose(0, 2, 1)]
    unnamed x6 -> x4, local copies, waits for them, and re-layouts: 0.02 us -> 2.01 us
    mul x1 -> x0, other arithmetic: 0.65 us -> none  [fused_body(): pixel_weight.astype(jnp.float32) * (camera - measured.astype(jnp.float32))]
where the time goes in v2:
time: 29.1 us; the launch traced here: 28.8 us
  Pallas kernels  26.2 us (90%)
  local copies, waits for them, and re-layouts  2.01 us (7%)
  between operations  0.65 us (2%)
    pallas_call x1, Pallas kernels, fused_body(): pl.pallas_call(functools.partial(kernel, frames, depths, row_shards), out...  26.2 us
    unnamed x4, local copies, waits for them, and re-layouts  2.01 us

profile of v2, /device:TPU:0, one launch (start us, length us, event | category | flops | bytes accessed | tf_op | source)
XLA Modules:
  0.0 28.8 jit_solution(11099474519640865032)
XLA Ops:
  0.6 26.2 %shard_map.68 = (f32[2,4608]{1,0:T(2,128)}, f32[2,4608]{1,0:T(2,128)}) custom-call(bf16[2,18432]{1,0:T(2,128)(2,1)} %bitcast.9, bf16[25,36,288]{2,1,0:T(8,128)(2,1)} %bitcast.8, s32[8,128]{1,0:T(8,128)} %region.1, bf16[2,4608]{1,0:T(2,128)(2,1)} %bitcast.13, s32[2,4608]{1,0:T(2,128)} %bitcast.10), custom_call_target="tpu_custom_call" | custom-call | tf_op jit(solution)/shard_map/pallas_call | solution.py:293
  26.8 0.0 copy-start
  26.8 1.4 %copy.9 = f32[1,2,4608]{2,1,0:T(2,128)} copy(f32[1,2,4608]{2,1,0:T(2,128)} %bitcast.12) | data formatting | bytes 73728
  28.2 0.0 copy-done
  28.2 0.6 %copy.10 = f32[1,2,4608]{2,1,0:T(2,128)} copy(f32[1,2,4608]{2,1,0:T(2,128)S(1)} %bitcast.11) | data formatting | bytes 73728
Async XLA Ops:
  26.8 1.4 %copy-start = (f32[2,4608]{1,0:T(2,128)S(1)}, f32[2,4608]{1,0:T(2,128)}, u32[]{:S(2)}) copy-start(f32[2,4608]{1,0:T(2,128)} %get-tuple-element.5) | copy-start | bytes 110596

commit v3 on v2

--- a/solution.py
+++ b/solution.py
@@ -187,7 +187,14 @@
                 xmask[top:top + phases, frame * cols:(frame + 1) * cols] = vol[frame, row] * keep
 
     lane = lax.broadcasted_iota(jnp.int32, (qpad, cols), 1)
-    x_copies = []
+    order = sorted(range(1, depths), key=lambda step: abs(step - depths // 2))
+    x_copies, z_copies = {}, {}
+
+    def frame_copy(quad, step):
+        share = lax.rem(me_d + step, depths)
+        return remote(part.at[other_f, quad, share], xrecv.at[quad, share], x_send.at[quad, step],
+                      x_recv.at[quad, step], x_dev)
+
     for quad in range(quads):
         sums = [[None] * frames for _ in range(depths)]
         for at in range(depths):
@@ -213,25 +220,26 @@
                     moved = pltpu.roll(sums[at][frame], shift, 1) if shift else sums[at][frame]
                     packed = moved if packed is None else jnp.where(lane >= at * col_share, moved, packed)
                 part[frame, quad, share] = packed
-        copy = remote(part.at[other_f, quad], xrecv.at[quad], x_send.at[quad], x_recv.at[quad], x_dev)
-        copy.start()
-        x_copies.append(copy)
-
-    z_copies = []
+        for step in order:
+            x_copies[quad, step] = frame_copy(quad, step)
+            x_copies[quad, step].start()
+
     for quad in range(quads):
-        x_copies[quad].wait_recv()
-        for share in range(depths):
-            zsend[quad, share] = part[me_f, quad, share] + xrecv[quad, share]
-        for step in range(1, depths):
+        x_copies[quad, 0] = frame_copy(quad, 0)
+        x_copies[quad, 0].start()
+    for quad in range(quads):
+        for step in order:
             to = lax.rem(me_d + step, depths)
-            copy = remote(zsend.at[quad, to], zrecv.at[quad, step - 1], z_send.at[quad, step - 1],
-                          z_recv.at[quad, step - 1], (me_f, to, me_r))
-            copy.start()
-            z_copies.append(copy)
+            x_copies[quad, step].wait_recv()
+            zsend[quad, to] = part[me_f, quad, to] + xrecv[quad, to]
+            z_copies[quad, step] = remote(zsend.at[quad, to], zrecv.at[quad, step - 1], z_send.at[quad, step - 1],
+                                          z_recv.at[quad, step - 1], (me_f, to, me_r))
+            z_copies[quad, step].start()
     for quad in range(quads):
-        total = zsend[quad, me_d]
-        for step in range(1, depths):
-            z_copies[quad * (depths - 1) + step - 1].wait_recv()
+        x_copies[quad, 0].wait_recv()
+        total = part[me_f, quad, me_d] + xrecv[quad, me_d]
+        for step in order:
+            z_copies[quad, step].wait_recv()
             total = total + zrecv[quad, step - 1]
         yred[quad] = total
 
@@ -270,7 +278,7 @@
     m_copy.wait()
     p_copy.wait()
     res[...] = praw[...].astype(jnp.float32) * (cam[...] - mraw[...].astype(jnp.float32))
-    for copy in (own_x, own_far, own_diag, own_core, fwd_x, fwd_far, fwd_diag, *x_copies, *z_copies, *y_copies):
+    for copy in (own_x, own_far, own_diag, own_core, fwd_x, fwd_far, fwd_diag, *x_copies.values(), *z_copies.values(), *y_copies):
         copy.wait_send()
 
 
@@ -281,7 +289,7 @@
     _, depth_rows, taps, width = point_spread.shape
     rows = rows_here * row_shards
     quads = rows // depths
-    qpad = round_up(width, 8)
+    qpad = width
     stride = round_up(width, 16)
     group = math.lcm(PHASES, 128) // PHASES
     span = group * PHASES
@@ -313,7 +321,7 @@
             pltpu.VMEM((quads, depths - 1, qpad, cols), jnp.float32),
             pltpu.VMEM((quads, qpad, cols), jnp.float32),
             pltpu.VMEM((row_shards, qpad, cols), jnp.float32),
-            dma, dma((7,)), dma((7,)), dma((quads,)), dma((quads,)),
+            dma, dma((7,)), dma((7,)), dma((quads, depths)), dma((quads, depths)),
             dma((quads, depths - 1)), dma((quads, depths - 1)),
             dma((row_shards - 1,)), dma((row_shards - 1,)),
         ],

time: 29.1 us -> 27.7 us (0.952)
  Pallas kernels: 26.2 us -> 24.8 us
    pallas_call x1, Pallas kernels: 26.2 us -> 24.8 us  [fused_body(): pl.pallas_call(functools.partial(kernel, frames, depths, row_shards), out...]
where the time goes in v3:
time: 27.7 us; the launch traced here: 27.5 us
  Pallas kernels  24.8 us (90%)
  local copies, waits for them, and re-layouts  2.01 us (7%)
  between operations  0.65 us (2%)
    pallas_call x1, Pallas kernels, fused_body(): pl.pallas_call(functools.partial(kernel, frames, depths, row_shards), out...  24.8 us
    unnamed x4, local copies, waits for them, and re-layouts  2.01 us

profile of v3, /device:TPU:0, one launch (start us, length us, event | category | flops | bytes accessed | tf_op | source)
XLA Modules:
  0.0 27.5 jit_solution(6558709768630768830)
XLA Ops:
  0.6 24.8 %shard_map.68 = (f32[2,4608]{1,0:T(2,128)}, f32[2,4608]{1,0:T(2,128)}) custom-call(bf16[2,18432]{1,0:T(2,128)(2,1)} %bitcast.9, bf16[25,36,288]{2,1,0:T(8,128)(2,1)} %bitcast.8, s32[8,128]{1,0:T(8,128)} %region.1, bf16[2,4608]{1,0:T(2,128)(2,1)} %bitcast.13, s32[2,4608]{1,0:T(2,128)} %bitcast.10), custom_call_target="tpu_custom_call" | custom-call | tf_op jit(solution)/shard_map/pallas_call | solution.py:301
  25.4 0.0 copy-start
  25.4 1.4 %copy.9 = f32[1,2,4608]{2,1,0:T(2,128)} copy(f32[1,2,4608]{2,1,0:T(2,128)} %bitcast.12) | data formatting | bytes 73728
  26.8 0.0 copy-done
  26.8 0.6 %copy.10 = f32[1,2,4608]{2,1,0:T(2,128)} copy(f32[1,2,4608]{2,1,0:T(2,128)S(1)} %bitcast.11) | data formatting | bytes 73728
Async XLA Ops:
  25.4 1.4 %copy-start = (f32[2,4608]{1,0:T(2,128)S(1)}, f32[2,4608]{1,0:T(2,128)}, u32[]{:S(2)}) copy-start(f32[2,4608]{1,0:T(2,128)} %get-tuple-element.5) | copy-start | bytes 110596

commit v4 on v3

--- a/solution.py
+++ b/solution.py
@@ -235,6 +235,11 @@
             z_copies[quad, step] = remote(zsend.at[quad, to], zrecv.at[quad, step - 1], z_send.at[quad, step - 1],
                                           z_recv.at[quad, step - 1], (me_f, to, me_r))
             z_copies[quad, step].start()
+    shares = row_shards // quads
+
+    def row_copy(to):
+        return remote(yred.at[to // shares], fin.at[me_r], y_send.at[to], y_recv.at[me_r], (me_f, me_d, to))
+
     for quad in range(quads):
         x_copies[quad, 0].wait_recv()
         total = part[me_f, quad, me_d] + xrecv[quad, me_d]
@@ -242,17 +247,17 @@
             z_copies[quad, step].wait_recv()
             total = total + zrecv[quad, step - 1]
         yred[quad] = total
-
-    shares = row_shards // quads
-    y_copies = []
-    for step in range(1, row_shards):
-        to = lax.rem(me_r + step, row_shards)
-        copy = remote(yred.at[to // shares], fin.at[me_r], y_send.at[step - 1], y_recv.at[step - 1], (me_f, me_d, to))
-        copy.start()
-        y_copies.append(copy)
+        for to in range(quad * shares, (quad + 1) * shares):
+            @pl.when(to != me_r)
+            def _():
+                row_copy(to).start()
     fin[me_r] = yred[me_r // shares]
-    for copy in y_copies:
-        copy.wait_recv()
+    for source in range(row_shards):
+        @pl.when(source != me_r)
+        def _():
+            remote(yred.at[0], fin.at[source], y_send.at[source], y_recv.at[source],
+                   (me_f, me_d, source)).wait_recv()
+            row_copy(source).wait_send()
     lanes_here = rows_here * col_share
     back = lax.rem(cols - lax.rem(me_r, shares) * lanes_here, cols)
     turned = jnp.concatenate(
@@ -278,7 +283,7 @@
     m_copy.wait()
     p_copy.wait()
     res[...] = praw[...].astype(jnp.float32) * (cam[...] - mraw[...].astype(jnp.float32))
-    for copy in (own_x, own_far, own_diag, own_core, fwd_x, fwd_far, fwd_diag, *x_copies.values(), *z_copies.values(), *y_copies):
+    for copy in (own_x, own_far, own_diag, own_core, fwd_x, fwd_far, fwd_diag, *x_copies.values(), *z_copies.values()):
         copy.wait_send()
 
 
@@ -323,7 +328,7 @@
             pltpu.VMEM((row_shards, qpad, cols), jnp.float32),
             dma, dma((7,)), dma((7,)), dma((quads, depths)), dma((quads, depths)),
             dma((quads, depths - 1)), dma((quads, depths - 1)),
-            dma((row_shards - 1,)), dma((row_shards - 1,)),
+            dma((row_shards,)), dma((row_shards,)),
         ],
         compiler_params=pltpu.CompilerParams(collective_id=0, has_side_effects=True),
     )(volume.reshape(rows_here, merged), spread, region_map, measured.reshape(image), pixel_weight.reshape(image))

time: 27.7 us -> 26.7 us (0.964)
  Pallas kernels: 24.8 us -> 23.8 us
    pallas_call x1, Pallas kernels: 24.8 us -> 23.8 us  [fused_body(): pl.pallas_call(functools.partial(kernel, frames, depths, row_shards), out...]
where the time goes in v4:
time: 26.7 us; the launch traced here: 26.5 us
  Pallas kernels  23.8 us (89%)
  local copies, waits for them, and re-layouts  2.01 us (8%)
  between operations  0.65 us (2%)
    pallas_call x1, Pallas kernels, fused_body(): pl.pallas_call(functools.partial(kernel, frames, depths, row_shards), out...  23.8 us
    unnamed x4, local copies, waits for them, and re-layouts  2.01 us

profile of v4, /device:TPU:0, one launch (start us, length us, event | category | flops | bytes accessed | tf_op | source)
XLA Modules:
  0.0 26.5 jit_solution(13392707557810668458)
XLA Ops:
  0.6 23.8 %shard_map.68 = (f32[2,4608]{1,0:T(2,128)}, f32[2,4608]{1,0:T(2,128)}) custom-call(bf16[2,18432]{1,0:T(2,128)(2,1)} %bitcast.9, bf16[25,36,288]{2,1,0:T(8,128)(2,1)} %bitcast.8, s32[8,128]{1,0:T(8,128)} %region.1, bf16[2,4608]{1,0:T(2,128)(2,1)} %bitcast.13, s32[2,4608]{1,0:T(2,128)} %bitcast.10), custom_call_target="tpu_custom_call" | custom-call | tf_op jit(solution)/shard_map/pallas_call | solution.py:306
  24.4 0.0 copy-start
  24.4 1.4 %copy.9 = f32[1,2,4608]{2,1,0:T(2,128)} copy(f32[1,2,4608]{2,1,0:T(2,128)} %bitcast.12) | data formatting | bytes 73728
  25.8 0.0 copy-done
  25.8 0.6 %copy.10 = f32[1,2,4608]{2,1,0:T(2,128)} copy(f32[1,2,4608]{2,1,0:T(2,128)S(1)} %bitcast.11) | data formatting | bytes 73728
Async XLA Ops:
  24.4 1.4 %copy-start = (f32[2,4608]{1,0:T(2,128)S(1)}, f32[2,4608]{1,0:T(2,128)}, u32[]{:S(2)}) copy-start(f32[2,4608]{1,0:T(2,128)} %get-tuple-element.5) | copy-start | bytes 110596

commit v5 on v4

--- a/solution.py
+++ b/solution.py
@@ -287,6 +287,11 @@
         copy.wait_send()
 
 
+def hand_over(camera_in, residual_in, camera_out, residual_out):
+    camera_out[...] = camera_in[...]
+    residual_out[...] = residual_in[...]
+
+
 def fused_body(sizes, volume, point_spread, region_map, measured, pixel_weight):
     frames, depths, row_shards = sizes
     _, _, rows_here, merged = volume.shape
@@ -332,6 +337,12 @@
         ],
         compiler_params=pltpu.CompilerParams(collective_id=0, has_side_effects=True),
     )(volume.reshape(rows_here, merged), spread, region_map, measured.reshape(image), pixel_weight.reshape(image))
+    camera, residual = pl.pallas_call(
+        hand_over,
+        out_shape=[jax.ShapeDtypeStruct(image, jnp.float32)] * 2,
+        in_specs=[vmem, vmem],
+        out_specs=[vmem, vmem],
+    )(camera, residual)
     return (camera.reshape(measured.shape), residual.reshape(measured.shape))
 
 

time: 26.7 us -> 26.1 us (0.978)
  local copies, waits for them, and re-layouts: 2.01 us -> 0 us
  Pallas kernels: 23.8 us -> 25.2 us
    unnamed x4 -> x0, local copies, waits for them, and re-layouts: 2.01 us -> none
    pallas_call x0 -> x1, Pallas kernels: none -> 1.42 us  [fused_body(): pl.pallas_call(hand_over, out_shape=[jax.ShapeDtypeStruct(image, jnp.floa...]
where the time goes in v5:
time: 26.1 us; the launch traced here: 25.9 us
  Pallas kernels  25.2 us (97%)
  between operations  0.64 us (2%)
    pallas_call x1, Pallas kernels, fused_body(): pl.pallas_call(functools.partial(kernel, frames, depths, row_shards), out...  23.8 us
    pallas_call x1, Pallas kernels, fused_body(): pl.pallas_call(hand_over, out_shape=[jax.ShapeDtypeStruct(image, jnp.floa...  1.42 us

profile of v5, /device:TPU:0, one launch (start us, length us, event | category | flops | bytes accessed | tf_op | source)
XLA Modules:
  0.0 25.9 jit_solution(7421782525129493069)
XLA Ops:
  0.6 23.8 %shard_map.68 = (f32[2,4608]{1,0:T(2,128)}, f32[2,4608]{1,0:T(2,128)}) custom-call(bf16[2,18432]{1,0:T(2,128)(2,1)} %bitcast.9, bf16[25,36,288]{2,1,0:T(8,128)(2,1)} %bitcast.8, s32[8,128]{1,0:T(8,128)} %region.1, bf16[2,4608]{1,0:T(2,128)(2,1)} %bitcast.11, s32[2,4608]{1,0:T(2,128)} %bitcast.10), custom_call_target="tpu_custom_call" | custom-call | tf_op jit(solution)/shard_map/pallas_call | solution.py:311
  24.4 1.4 %shard_map.69 = (f32[2,4608]{1,0:T(2,128)}, f32[2,4608]{1,0:T(2,128)}) custom-call(f32[2,4608]{1,0:T(2,128)} %get-tuple-element.6.camera_in, f32[2,4608]{1,0:T(2,128)} %get-tuple-element.7.residual_in), custom_call_target="tpu_custom_call" | custom-call | tf_op jit(solution)/shard_map/pallas_call | solution.py:340

commit v6 on v5

--- a/solution.py
+++ b/solution.py
@@ -103,8 +103,8 @@
             vin[row, half * 128:half * 128 + count, :] = turned[:count].astype(jnp.bfloat16)
 
 
-def kernel(frames, depths, row_shards, v_hbm, w_hbm, region, m_hbm, p_hbm, cam, res, raw, wide, pieces, vin,
-           mraw, praw, in_sem, vol, wraw, wflat, xmask, part, xrecv, zsend,
+def kernel(frames, depths, row_shards, v_hbm, w_hbm, region, cam, raw, wide, pieces, vin,
+           in_sem, vol, wraw, wflat, xmask, part, xrecv, zsend,
            zrecv, yred, fin, w_sem, g_send, g_recv, x_send, x_recv, z_send, z_recv, y_send, y_recv):
     reach = TAP_SIDE // 2
     rows_here, phases, cols = vin.shape
@@ -136,10 +136,6 @@
     v_copy.start()
     w_copy = pltpu.make_async_copy(w_hbm, wraw, w_sem)
     w_copy.start()
-    m_copy = pltpu.make_async_copy(m_hbm, mraw, in_sem.at[1])
-    m_copy.start()
-    p_copy = pltpu.make_async_copy(p_hbm, praw, in_sem.at[2])
-    p_copy.start()
     v_copy.wait()
     lanes_from_rows(raw, wide, pieces, vin)
     pl.semaphore_wait(barrier, len(partners))
@@ -280,16 +276,13 @@
         for at in range(per_row):
             line = row * per_row + at
             cam[row:row + 1, at * span:(at + 1) * span] = strips[line:line + 1]
-    m_copy.wait()
-    p_copy.wait()
-    res[...] = praw[...].astype(jnp.float32) * (cam[...] - mraw[...].astype(jnp.float32))
     for copy in (own_x, own_far, own_diag, own_core, fwd_x, fwd_far, fwd_diag, *x_copies.values(), *z_copies.values()):
         copy.wait_send()
 
 
-def hand_over(camera_in, residual_in, camera_out, residual_out):
+def hand_over(camera_in, recorded, weight, camera_out, residual_out):
     camera_out[...] = camera_in[...]
-    residual_out[...] = residual_in[...]
+    residual_out[...] = weight[...].astype(jnp.float32) * (camera_in[...] - recorded[...].astype(jnp.float32))
 
 
 def fused_body(sizes, volume, point_spread, region_map, measured, pixel_weight):
@@ -308,19 +301,17 @@
     vmem = pl.BlockSpec(memory_space=pltpu.VMEM)
     hbm = pl.BlockSpec(memory_space=pl.ANY)
     dma = pltpu.SemaphoreType.DMA
-    camera, residual = pl.pallas_call(
+    camera = pl.pallas_call(
         functools.partial(kernel, frames, depths, row_shards),
-        out_shape=[jax.ShapeDtypeStruct(image, jnp.float32)] * 2,
-        in_specs=[hbm, hbm, vmem, hbm, hbm],
-        out_specs=[vmem, vmem],
+        out_shape=jax.ShapeDtypeStruct(image, jnp.float32),
+        in_specs=[hbm, hbm, vmem],
+        out_specs=vmem,
         scratch_shapes=[
             pltpu.VMEM((rows_here, merged), jnp.bfloat16),
             pltpu.VMEM((rows_here * cols // group, span + 128), jnp.float32),
             pltpu.VMEM((round_up(PHASES, 128) // 128, rows_here * cols, 128), jnp.float32),
             pltpu.VMEM((rows_here, PHASES, cols), jnp.bfloat16),
-            pltpu.VMEM(image, jnp.bfloat16),
-            pltpu.VMEM(image, jnp.int32),
-            dma((3,)),
+            dma((1,)),
             pltpu.VMEM((frames, rows, PHASES, cols), jnp.bfloat16),
             pltpu.VMEM((taps, width, depth_rows), jnp.bfloat16),
             pltpu.VMEM((TAP_SIDE * stride, TAP_SIDE * depth_rows), jnp.bfloat16),
@@ -336,13 +327,13 @@
             dma((row_shards,)), dma((row_shards,)),
         ],
         compiler_params=pltpu.CompilerParams(collective_id=0, has_side_effects=True),
-    )(volume.reshape(rows_here, merged), spread, region_map, measured.reshape(image), pixel_weight.reshape(image))
+    )(volume.reshape(rows_here, merged), spread, region_map)
     camera, residual = pl.pallas_call(
         hand_over,
         out_shape=[jax.ShapeDtypeStruct(image, jnp.float32)] * 2,
-        in_specs=[vmem, vmem],
+        in_specs=[vmem] * 3,
         out_specs=[vmem, vmem],
-    )(camera, residual)
+    )(camera, measured.reshape(image), pixel_weight.reshape(image))
     return (camera.reshape(measured.shape), residual.reshape(measured.shape))
 
 

time: 26.1 us -> 26.1 us (level)
  no operation moved by 1% of the time
where the time goes in v6:
time: 26.1 us; the launch traced here: 25.8 us
  Pallas kernels  25.2 us (97%)
  between operations  0.64 us (2%)
    pallas_call x1, Pallas kernels, fused_body(): pl.pallas_call(functools.partial(kernel, frames, depths, row_shards), out...  23.8 us
    pallas_call x1, Pallas kernels, fused_body(): pl.pallas_call(hand_over, out_shape=[jax.ShapeDtypeStruct(image, jnp.floa...  1.44 us

profile of v6, /device:TPU:0, one launch (start us, length us, event | category | flops | bytes accessed | tf_op | source)
XLA Modules:
  0.0 25.8 jit_solution(2873842803906433701)
XLA Ops:
  0.6 23.8 %shard_map.68.camera_in = f32[2,4608]{1,0:T(2,128)} custom-call(bf16[2,18432]{1,0:T(2,128)(2,1)} %bitcast.9, bf16[25,36,288]{2,1,0:T(8,128)(2,1)} %bitcast.8, s32[8,128]{1,0:T(8,128)} %region.1), custom_call_target="tpu_custom_call" | custom-call | tf_op jit(solution)/shard_map/pallas_call | solution.py:304
  24.4 1.4 %shard_map.69 = (f32[2,4608]{1,0:T(2,128)}, f32[2,4608]{1,0:T(2,128)}) custom-call(f32[2,4608]{1,0:T(2,128)} %shard_map.68.camera_in, bf16[2,4608]{1,0:T(2,128)(2,1)} %bitcast.11, s32[2,4608]{1,0:T(2,128)} %bitcast.10), custom_call_target="tpu_custom_call" | custom-call | tf_op jit(solution)/shard_map/pallas_call | solution.py:331
